TPU v7x, 256 devices: a whole 4x4x8 slice. The times are simulated.
256 devices in a mesh: seq: 32 (over y_hi, z, core), head: 8 (over y_lo, x).
Axes of the slice: x: 4, y: 4 (y_hi: 2, y_lo: 2; y = y_hi * 2 + y_lo), z: 8, core: 2. Of those that a mesh axis runs over, the one named last changes fastest.
Arguments:
- q_cells: bfloat16 [8192, 8192], P('seq', 'head'), may hold values from -60 to 60
- k_cells: bfloat16 [8192, 1024], P('seq', 'head'), may hold values from -11 to 11
- v_cells: bfloat16 [8192, 1024], P('seq', 'head'), may hold values from -6 to 6
- do_cells: bfloat16 [8192, 8192], P('seq', 'head'), may hold values from -6 to 6
- q_head: bfloat16 [1024, 8192], P('seq', 'head'), may hold values from -60 to 60
- k_head: bfloat16 [1024, 1024], P('seq', 'head'), may hold values from -6 to 6
- v_head: bfloat16 [1024, 1024], P('seq', 'head'), may hold values from -6 to 6
- do_head: bfloat16 [1024, 8192], P('seq', 'head'), may hold values from -6 to 6
- vis_mask: int32 [64, 8], P('seq'), may hold values from 0 to 1, as said below
Outputs:
- dq_cells: bfloat16 [8192, 8192], P('seq', 'head')
- dk_cells: bfloat16 [8192, 1024], P('seq', 'head')
- dv_cells: bfloat16 [8192, 1024], P('seq', 'head')
- dq_head: bfloat16 [1024, 8192], P('seq', 'head')
- dk_head: bfloat16 [1024, 1024], P('seq', 'head')
- dv_head: bfloat16 [1024, 1024], P('seq', 'head')
Inputs may be any that keep to these rules, and one draw needn't show every extreme that they name: vis_mask[b, t] = 1 lets the cells of block b see the headers of block t.
All inputs are finite; a program needn't handle non-finite values.
Results may differ from a plain program's by a relative error of at most 0.012.
Values may be sent and summed in bfloat16 or wider, within the bound.
A program may use at most 64 MiB of HBM per device.

v0:
```python
from functools import partial
import jax
import jax.numpy as jnp
from jax import lax
from jax.sharding import PartitionSpec as P

HD = 128
W = 256
BLOCK = 128
masked_score = -1e30


def product(pattern, former, latter):
    return jnp.einsum(pattern, former, latter, preferred_element_type=jnp.float32)


def block_stats(queries, key_rows, visible, scaling):
    scores = product("nkgd,mkd->kgnm", queries, key_rows) * scaling
    kept_scores = jnp.where(visible, scores, masked_score)
    highest = jnp.max(kept_scores, axis=-1)
    totals = jnp.sum(jnp.where(visible, jnp.exp(scores - highest[..., None]), 0.0), axis=-1)
    return (highest, totals)


def merge_stats(former, latter):
    highest = jnp.maximum(former[0], latter[0])
    return (
        highest,
        former[1] * jnp.exp(former[0] - highest) + latter[1] * jnp.exp(latter[0] - highest),
    )


def weights_of(queries, key_rows, log_totals, visible, scaling):
    scores = product("nkgd,mkd->kgnm", queries, key_rows) * scaling
    return jnp.where(visible, jnp.exp(scores - log_totals[..., None]), 0.0)


def block_delta(queries, grads_out, key_rows, value_rows, log_totals, visible, scaling):
    weights = weights_of(queries, key_rows, log_totals, visible, scaling)
    slopes = product("nkgd,mkd->kgnm", grads_out, value_rows)
    return jnp.sum(weights * slopes, axis=-1)


def block_grads(queries, grads_out, key_rows, value_rows, log_totals, deltas, visible, scaling):
    weights = weights_of(queries, key_rows, log_totals, visible, scaling)
    slopes = product("nkgd,mkd->kgnm", grads_out, value_rows)
    score_grads = weights * (slopes - deltas[..., None])
    weight_low = weights.astype(jnp.bfloat16)
    grad_low = score_grads.astype(jnp.bfloat16)
    grad_values = product("kgnm,nkgd->mkd", weight_low, grads_out)
    grad_keys = product("kgnm,nkgd->mkd", grad_low, queries) * scaling
    grad_queries = product("kgnm,mkd->nkgd", grad_low, key_rows) * scaling
    return (grad_queries, grad_keys, grad_values)


def to_rows(values):
    return jnp.transpose(values, (1, 2, 0, 3)).reshape(values.shape[1], values.shape[2], -1)


def from_rows(values, pieces):
    return jnp.transpose(values.reshape(values.shape[0], values.shape[1], pieces, -1), (2, 0, 1, 3))


def guarded(function, operands):
    return function(*operands)


def per_device(q_cells, k_cells, v_cells, do_cells, q_head, k_head, v_head, do_head, vis_mask):
    cell_count = q_cells.shape[0]
    kv_local = k_cells.shape[1] // HD
    query_local = q_cells.shape[1] // HD
    groups = query_local // kv_local
    scaling = HD ** (-0.5)
    regions = cell_count // W
    own_rows = q_head.shape[0]
    head_keys, head_values = (
        lax.all_gather(k_head, "seq", axis=0, tiled=True),
        lax.all_gather(v_head, "seq", axis=0, tiled=True),
    )
    all_queries, all_grads = (
        lax.all_gather(q_head, "seq", axis=0, tiled=True),
        lax.all_gather(do_head, "seq", axis=0, tiled=True),
    )
    header_count = head_keys.shape[0]
    blocks = header_count // BLOCK
    cell_query = q_cells.reshape(cell_count, kv_local, groups, HD)
    cell_grad = do_cells.reshape(cell_count, kv_local, groups, HD)
    cell_key = k_cells.reshape(cell_count, kv_local, HD)
    cell_value = v_cells.reshape(cell_count, kv_local, HD)
    region_query = q_cells.reshape(regions, W, kv_local, groups, HD)
    region_grad = do_cells.reshape(regions, W, kv_local, groups, HD)
    region_key = k_cells.reshape(regions, W, kv_local, HD)
    region_value = v_cells.reshape(regions, W, kv_local, HD)
    header_key_rows = head_keys.reshape(header_count, kv_local, HD)
    header_value_rows = head_values.reshape(header_count, kv_local, HD)
    key_blocks = head_keys.reshape(blocks, BLOCK, kv_local, HD)
    value_blocks = head_values.reshape(blocks, BLOCK, kv_local, HD)
    seen_blocks = jnp.transpose(jnp.repeat(vis_mask, BLOCK, axis=0) > 0)

    def outer_stat(operands):
        key_block, seen_column = operands
        return guarded(
            partial(block_stats, cell_query, scaling=scaling), (key_block, seen_column[:, None])
        )

    block_highest, block_totals = lax.map(outer_stat, (key_blocks, seen_blocks))
    outer_highest = jnp.max(block_highest, axis=0)
    outer_totals = jnp.sum(block_totals * jnp.exp(block_highest - outer_highest), axis=0)
    local_stats = jax.vmap(partial(block_stats, visible=True, scaling=scaling))(
        region_query, region_key
    )
    highest, totals = merge_stats(
        (to_rows(local_stats[0]), to_rows(local_stats[1])), (outer_highest, outer_totals)
    )
    cell_log = highest + jnp.log(totals)
    region_log = from_rows(cell_log, regions)

    def outer_delta(operands):
        key_block, value_block, seen_column = operands
        return guarded(
            partial(block_delta, cell_query, cell_grad, scaling=scaling),
            (key_block, value_block, cell_log, seen_column[:, None]),
        )

    local_delta = to_rows(
        jax.vmap(partial(block_delta, visible=True, scaling=scaling))(
            region_query, region_grad, region_key, region_value, region_log
        )
    )
    cell_delta = local_delta + jnp.sum(
        lax.map(outer_delta, (key_blocks, value_blocks, seen_blocks)), axis=0
    )
    query_zeros = jnp.zeros((cell_count, kv_local, groups, HD), jnp.float32)

    def outer_grad(running, operands):
        key_block, value_block, seen_column = operands
        gradients = guarded(
            partial(block_grads, cell_query, cell_grad, scaling=scaling),
            (key_block, value_block, cell_log, cell_delta, seen_column[:, None]),
        )
        return (running + gradients[0], (gradients[1], gradients[2]))

    outer_query, (key_parts, value_parts) = lax.scan(
        outer_grad, query_zeros, (key_blocks, value_blocks, seen_blocks)
    )
    local_grads = jax.vmap(partial(block_grads, visible=True, scaling=scaling))(
        region_query,
        region_grad,
        region_key,
        region_value,
        region_log,
        from_rows(cell_delta, regions),
    )
    query_blocks = all_queries.reshape(blocks, BLOCK, kv_local, groups, HD)
    grad_blocks = all_grads.reshape(blocks, BLOCK, kv_local, groups, HD)
    own_query = q_head.reshape(own_rows, kv_local, groups, HD)
    own_grad = do_head.reshape(own_rows, kv_local, groups, HD)
    first_row = lax.axis_index("seq") * own_rows

    def own_slice(values):
        return lax.dynamic_slice_in_dim(values, first_row, own_rows, 2)

    def own_update(values, replaced):
        return lax.dynamic_update_slice_in_dim(values, replaced, first_row, 2)

    cross_stats = lax.map(
        lambda operands: block_stats(operands, cell_key, True, scaling), query_blocks
    )
    cross_highest = to_rows(cross_stats[0])
    cross_totals = to_rows(cross_stats[1])
    self_stats = block_stats(own_query, header_key_rows, True, scaling)
    own_merged = merge_stats((own_slice(cross_highest), own_slice(cross_totals)), self_stats)
    part_highest = own_update(cross_highest, own_merged[0])
    part_totals = own_update(cross_totals, own_merged[1])
    head_highest = lax.pmax(part_highest.astype(jnp.bfloat16), "seq").astype(part_highest.dtype)
    head_totals = lax.psum(part_totals * jnp.exp(part_highest - head_highest), "seq")
    head_log = head_highest + jnp.log(head_totals)
    block_log = from_rows(head_log, blocks)
    own_log = own_slice(head_log)
    cross_delta = to_rows(
        lax.map(
            lambda operands: block_delta(
                operands[0], operands[1], cell_key, cell_value, operands[2], True, scaling
            ),
            (query_blocks, grad_blocks, block_log),
        )
    )
    self_delta = block_delta(
        own_query, own_grad, header_key_rows, header_value_rows, own_log, True, scaling
    )
    part_delta = own_update(cross_delta, own_slice(cross_delta) + self_delta)
    head_delta = lax.psum(part_delta, "seq")
    block_deltas = from_rows(head_delta, blocks)
    own_delta = own_slice(head_delta)
    key_zeros = jnp.zeros((cell_count, kv_local, HD), jnp.float32)

    def cross_grad(running, operands):
        gradients = block_grads(
            operands[0], operands[1], cell_key, cell_value, operands[2], operands[3], True, scaling
        )
        return ((running[0] + gradients[1], running[1] + gradients[2]), gradients[0])

    (cross_key, cross_value), cross_query = lax.scan(
        cross_grad, (key_zeros, key_zeros), (query_blocks, grad_blocks, block_log, block_deltas)
    )
    self_grads = block_grads(
        own_query, own_grad, header_key_rows, header_value_rows, own_log, own_delta, True, scaling
    )
    query_part = cross_query.reshape(header_count, query_local * HD)
    key_part = key_parts.reshape(header_count, kv_local * HD) + self_grads[1].reshape(
        header_count, kv_local * HD
    )
    value_part = value_parts.reshape(header_count, kv_local * HD) + self_grads[2].reshape(
        header_count, kv_local * HD
    )
    whole_sums = lax.psum((query_part, key_part, value_part), "seq")
    query_sum, key_sum, value_sum = [
        lax.dynamic_slice_in_dim(summed, first_row, own_rows, 0) for summed in whole_sums
    ]
    dq_cells = (
        local_grads[0].reshape(cell_count, query_local * HD)
        + outer_query.reshape(cell_count, query_local * HD)
    ).astype(jnp.bfloat16)
    dk_cells = (
        local_grads[1].reshape(cell_count, kv_local * HD)
        + cross_key.reshape(cell_count, kv_local * HD)
    ).astype(jnp.bfloat16)
    dv_cells = (
        local_grads[2].reshape(cell_count, kv_local * HD)
        + cross_value.reshape(cell_count, kv_local * HD)
    ).astype(jnp.bfloat16)
    dq_head = (query_sum + self_grads[0].reshape(own_rows, query_local * HD)).astype(jnp.bfloat16)
    return (
        dq_cells,
        dk_cells,
        dv_cells,
        dq_head,
        key_sum.astype(jnp.bfloat16),
        value_sum.astype(jnp.bfloat16),
    )


def solution(mesh):
    return jax.shard_map(
        per_device,
        mesh=mesh,
        in_specs=(
            P("seq", "head"),
            P("seq", "head"),
            P("seq", "head"),
            P("seq", "head"),
            P("seq", "head"),
            P("seq", "head"),
            P("seq", "head"),
            P("seq", "head"),
            P("seq", None),
        ),
        out_specs=(
            P("seq", "head"),
            P("seq", "head"),
            P("seq", "head"),
            P("seq", "head"),
            P("seq", "head"),
            P("seq", "head"),
        ),
        check_vma=False,
    )
```

profile of v0, /device:TPU:1, one launch (start us, length us, event | category | flops | bytes accessed | tf_op | source)
XLA Modules:
  0.0 988.0 jit_solution(11837171689813258582)
XLA Ops:
  9.5 47.2 %all_gather.12 = bf16[1024,128]{1,0:T(8,128)(2,1)S(1)} all-gather(bf16[32,128]{1,0:T(8,128)(2,1)} %param.26), channel_id=1, replica_groups=mesh['seq'=32,'head'=8] {'seq'}, dimensions={0}, use_global_device_ids=true | all-gather | bytes 270336 | tf_op jit(solution)/shard_map/all_gather | solution.py:77
  56.7 40.4 %all_gather.13 = bf16[1024,128]{1,0:T(8,128)(2,1)} all-gather(bf16[32,128]{1,0:T(8,128)(2,1)} %param.27), channel_id=1, replica_groups=mesh['seq'=32,'head'=8] {'seq'}, dimensions={0}, use_global_device_ids=true | all-gather | bytes 270336 | tf_op jit(solution)/shard_map/all_gather | solution.py:78
  98.7 4.6 while.74
  104.2 1.5 bitcast_reduce_fusion
  109.0 16.5 %while.75 = (s32[]{:T(128)}, f32[8,1,8,256]{3,2,1,0:T(8,128)}, pred[8,256]{1,0:T(8,128)(4,1)S(1)}, bf16[8,128,1,128]{3,1,2,0:T(8,128)(2,1)S(1)}, bf16[256,1,8,12...) while((s32[]{:T(128)}, f32[8,1,8,256]{3,2,1,0:T(8,128)}, ...), condition=%wide.region_11.12_spmd, body=%wide.region_9.11_spmd.sunk | while | flops 135526400 | bytes 3245173 | solution.py:131
  125.5 1.4 reduce_sum.103
  127.8 3.0 fusion.95
  133.0 2.2 copy.97
  135.3 1.9 copy.67
  137.2 37.2 %all-gather.5.cloned.1.call-done = bf16[1024,1024]{1,0:T(8,128)(2,1)} async-done(((bf16[32,1024]{1,0:T(8,128)(2,1)}), bf16[1024,1024]{1,0:T(8,128)(2,1)}) %all-gather.5.cloned.1.call-update) | async-done | bytes 2097168 | tf_op jit(solution)/shard_map/all_gather | solution.py:82
  174.4 2.2 copy.98
  176.6 1.9 copy.68
  179.8 18.8 %while.76 = (s32[]{:T(128)}, f32[8,1,8,128]{3,2,1,0:T(8,128)}, f32[8,1,8,128]{3,2,1,0:T(8,128)}, bf16[8,128,1,8,128]{4,1,3,2,0:T(8,128)(2,1)}, bf16[256,1,128]{2,0,1:T(8,128)(2,1)S(1)}, /*index=5*/s32[]{:T(128)}) while((s32[]{:T(128)}, f32[8,1,8,128]{3,2,1,0:T(8,128)}, f32[8,1,8,128]{3,2,1,0:T(8,128)}, ...), condition=%wide.region_18.19_spmd, body=%wide.region_15.18_spmd.sunk | while | flops 68155392 | bytes 2453589 | solution.py:166
  179.8 1.4 fusion.227
  182.1 1.3 fusion.227
  184.5 1.3 fusion.227
  186.8 1.4 fusion.227
  189.1 1.3 fusion.227
  191.5 1.3 fusion.227
  193.8 1.3 fusion.227
  196.2 1.4 fusion.227
  198.5 1.4 fusion.157
  199.9 1.5 dynamic_update_slice.41
  201.4 1.5 dynamic_update_slice.40
  202.8 1.4 convert_element_type.50
  204.2 124.3 %pmax.7 = bf16[1,8,1024]{2,1,0:T(8,128)(2,1)} all-reduce(bf16[1,8,1024]{2,1,0:T(8,128)(2,1)} %convert_element_type.50), channel_id=1, replica_groups=mesh['seq'=32,'head'=8] {'seq'}, use_global_device_ids=true, to_apply=%region_20.21 | all-reduce | flops 8192 | bytes 32768 | tf_op jit(solution)/shard_map/pmax | solution.py:175
  328.5 1.4 fusion.148
  329.9 128.5 %psum.35 = f32[1,8,1024]{2,1,0:T(8,128)} all-reduce(f32[1,8,1024]{2,1,0:T(8,128)} %fusion.148), channel_id=1, replica_groups=mesh['seq'=32,'head'=8] {'seq'}, use_global_device_ids=true, to_apply=%region_22.23 | all-reduce | flops 8192 | bytes 65536 | tf_op jit(solution)/shard_map/psum | solution.py:176
  460.5 31.5 %while.77 = (s32[]{:T(128)}, f32[8,1,8,128]{3,2,1,0:T(8,128)}, bf16[8,128,1,8,128]{4,1,3,2,0:T(8,128)(2,1)}, bf16[256,1,128]{2,0,1:T(8,128)(2,1)S(1)}, f32[8,1,8...) while((s32[]{:T(128)}, f32[8,1,8,128]{3,2,1,0:T(8,128)}, ...), condition=%wide.region_25.26_spmd, body=%wide.region_23.25_spmd.sunk | while | flops 135265280 | bytes 2777197 | solution.py:181
  462.4 1.4 fusion.233
  466.4 1.4 fusion.233
  470.3 1.4 fusion.233
  474.2 1.4 fusion.233
  478.2 1.4 fusion.233
  482.1 1.4 fusion.233
  486.0 1.4 fusion.233
  490.0 1.4 fusion.233
  491.9 2.6 multiply_reduce_fusion
  494.5 1.4 bitcast_add_fusion.1
  495.9 1.5 dynamic_update_slice.42
  497.3 128.5 %psum.36 = f32[1,8,1024]{2,1,0:T(8,128)} all-reduce(f32[1,8,1024]{2,1,0:T(8,128)} %dynamic_update_slice.42), channel_id=1, replica_groups=mesh['seq'=32,'head'=8] {'seq'}, use_global_device_ids=true, to_apply=%region_27.28 | all-reduce | flops 8192 | bytes 65536 | tf_op jit(solution)/shard_map/psum | solution.py:192
  625.9 63.3 %while.79 = (s32[]{:T(128)}, f32[256,1,128]{0,2,1:T(8,128)}, f32[256,1,128]{0,2,1:T(8,128)}, f32[8,128,1,8,128]{4,3,1,0,2:T(8,128)}, bf16[8,128,1,8,128]{4,1,3,2...) while((s32[]{:T(128)}, f32[256,1,128]{0,2,1:T(8,128)}, ...), condition=%wide.region_29.30_spmd.clone, body=%wide.region_28.29_spmd.clone.sunk | while | flops 337412096 | bytes 9134296 | solution.py:203
  627.9 1.9 fusion.262
  635.8 1.9 fusion.262
  642.4 1.3 fusion.259
  643.7 1.9 fusion.262
  650.3 1.3 fusion.259
  651.6 1.9 fusion.262
  658.2 1.3 fusion.259
  659.5 1.9 fusion.262
  667.4 1.9 fusion.262
  675.4 1.9 fusion.262
  683.3 1.9 fusion.262
  689.2 5.1 copy.144
  694.9 39.1 %while.78 = (s32[]{:T(128)}, f32[256,1,8,128]{0,3,2,1:T(8,128)}, f32[8,128,1,128]{3,1,2,0:T(8,128)}, f32[8,128,1,128]{3,1,2,0:T(8,128)}, bf16[8,128,1,128]{3,1,2...) while((s32[]{:T(128)}, f32[256,1,8,128]{0,3,2,1:T(8,128)}, ...), condition=%wide.region_14.15_spmd.clone, body=%wide.region_13.14_spmd.clone.sunk | while | flops 338182144 | bytes 17548512 | solution.py:143
  734.1 2.5 copy.83
  736.6 2.1 fusion.114
  738.7 1.4 convolution_multiply_fusion.8
  740.1 2.5 copy.60
  742.7 2.6 add_convert_fusion
  749.5 140.0 %all-reduce.5 = (bf16[1024,128]{1,0:T(8,128)(2,1)S(1)}, bf16[1024,128]{1,0:T(8,128)(2,1)}) all-reduce(f32[1024,128]{1,0:T(8,128)} %fusion.104, f32[1024,128]{1,0:T(8,128)} %fusion.105), channel_id=1, replica_groups=mesh['seq'=32,'head'=8] {'seq'}, use_global_device_ids=true, to_apply=%region_31.32 | all-reduce | flops 262144 | bytes 1572864 | tf_op jit(solution)/shard_map/psum | solution.py:216
  890.8 2.4 fusion.111
  894.4 85.6 %all-reduce.4.cloned.1.call-done = f32[1024,1024]{1,0:T(8,128)} async-done(((f32[1024,1024]{1,0:T(8,128)}), f32[1024,1024]{1,0:T(8,128)}) %all-reduce.4.cloned.1.call-update) | async-done | bytes 4194320 | tf_op jit(solution)/shard_map/psum | solution.py:216
  979.9 1.6 fusion.135
  (362 shorter events, 153.0 us)
Async XLA Ops:
  7.2 125.9 %all-gather.3.cloned.1.call-start = ((), (), s32[]{:S(2)}) async-start(), calls=%async_computation | async-start | bytes 2162688 | tf_op jit(solution)/shard_map/all_gather | solution.py:81
  7.9 166.5 %all-gather.5.cloned.1.call-start = ((), (), s32[]{:S(2)}) async-start(), calls=%async_computation.1 | async-start | bytes 2162688 | tf_op jit(solution)/shard_map/all_gather | solution.py:82
  8.6 971.3 %all-reduce.4.cloned.1.call-start = ((), (), s32[]{:S(2)}) async-start(), calls=%async_computation.2 | async-start | bytes 8388608 | tf_op jit(solution)/shard_map/psum | solution.py:216
  98.7 4.6 copy-start.9
  103.3 0.6 copy-start.15
  103.3 0.9 copy-start.2
  105.7 1.5 copy-start.23
  106.4 1.3 copy-start.24
  107.2 1.8 copy-start.26
  107.6 1.4 copy-start.25
  109.0 18.7 %copy-start.5 = (bf16[256,128]{1,0:T(8,128)(2,1)S(1)}, bf16[256,128]{1,0:T(8,128)(2,1)}, u32[]{:S(2)}) copy-start(bf16[256,128]{1,0:T(8,128)(2,1)} %param.23) | copy-start | bytes 196612
  125.5 5.2 copy-start.19
  127.8 3.0 copy-start.21
  127.8 3.0 copy-start.29
  127.8 3.0 copy-start.16
  131.2 1.0 copy-start.3
  131.2 1.0 copy-start.27
  459.2 1.3 copy-start.18
  626.6 4.5 copy-start.6
  632.3 1.4 copy-start.7
  634.5 4.5 copy-start.6
  640.2 1.4 copy-start.7
  642.4 4.5 copy-start.6
  648.2 1.4 copy-start.7
  650.3 4.5 copy-start.6
  656.1 1.4 copy-start.7
  658.2 4.5 copy-start.6
  664.0 1.4 copy-start.7
  666.1 4.5 copy-start.6
  671.9 1.4 copy-start.7
  674.1 4.5 copy-start.6
  679.8 1.4 copy-start.7
  682.0 4.5 copy-start.6
  687.7 1.4 copy-start.7
  694.3 0.7 copy-start.20
  695.3 3.0 copy-start
  698.8 1.1 copy-start.1
  700.2 3.0 copy-start
  703.7 1.1 copy-start.1
  705.1 3.0 copy-start
  708.6 1.1 copy-start.1
  710.0 3.0 copy-start
  713.5 1.1 copy-start.1
  714.9 3.0 copy-start
  718.3 1.1 copy-start.1
  719.8 3.0 copy-start
  723.2 1.1 copy-start.1
  724.7 3.0 copy-start
  728.1 1.1 copy-start.1
  729.6 3.0 copy-start
  733.0 1.1 copy-start.1
  734.1 2.5 copy-start.22
  738.7 1.4 copy-start.12
  740.1 6.0 copy-start.28
  742.7 3.5 copy-start.4
  742.7 3.5 copy-start.13
  745.3 1.5 copy-start.17
  745.3 1.5 copy-start.31
  746.4 1.6 copy-start.14
  746.5 1.6 copy-start.30
  746.9 2.4 copy-start.8
  746.9 2.5 copy-start.11
  749.3 143.9 %copy-start.10 = (bf16[256,1024]{1,0:T(8,128)(2,1)S(1)}, bf16[256,1024]{1,0:T(8,128)(2,1)}, u32[]{:S(2)}) copy-start(bf16[256,1024]{1,0:T(8,128)(2,1)} %param.24) | copy-start | bytes 1572868
Sparse Core Ops, SparseCore 0:
  10.8 84.3 all-gather.2
  98.0 76.3 all-gather.4
  694.4 285.4 all-reduce.3
where the time goes:
time: 992 us; the launch traced here: 988 us
  blocking collectives  609 us (61%)
  matrix products  139 us (14%)
  waiting for transfers between devices  124 us (12%)
  local copies, waits for them, and re-layouts  76.3 us (8%)
  other arithmetic  23.8 us (2%)
  between operations  14.2 us (1%)
    psum x1, blocking collectives, per_device(): whole_sums = lax.psum((query_part, key_part, value_part), 'seq')  140 us
    dot_general x138, matrix products, product(): jnp.einsum(pattern, former, latter, preferred_element_type=jnp.float32)  139 us
    psum x1, blocking collectives, per_device(): head_delta = lax.psum(part_delta, 'seq')  129 us
    psum x1, blocking collectives, per_device(): lax.psum(part_totals * jnp.exp(part_highest - head_highest), 'seq')  128 us
    pmax x1, blocking collectives, per_device(): lax.pmax(part_highest.astype(jnp.bfloat16), 'seq')  124 us
    psum x1, waiting for transfers between devices, per_device(): whole_sums = lax.psum((query_part, key_part, value_part), 'seq')  85.6 us
    all_gather x1, blocking collectives, per_device(): lax.all_gather(k_head, 'seq', axis=0, tiled=True)  47.2 us
    all_gather x1, blocking collectives, per_device(): lax.all_gather(v_head, 'seq', axis=0, tiled=True)  40.4 us
  transfers between devices with their start and end apart: 3, of which 2 were waited for; matrix products, arithmetic and copies ran while one was open for 9% of the time, Pallas kernels for 0%

commit v1 on v0

--- a/solution.py
+++ b/solution.py
@@ -75,7 +75,9 @@
     own_rows = q_head.shape[0]
     head_keys, head_values = (
         lax.all_gather(k_head, "seq", axis=0, tiled=True),
-        lax.all_gather(v_head, "seq", axis=0, tiled=True),
+        jnp.concatenate(
+            lax.all_to_all(jnp.stack([v_head] * lax.axis_size("seq")), "seq", 0, 0), axis=0
+        ),
     )
     all_queries, all_grads = (
         lax.all_gather(q_head, "seq", axis=0, tiled=True),

time: 992 us -> 992 us (level)
  blocking collectives: 609 us -> 564 us
  waiting for transfers between devices: 124 us -> 147 us
  starting transfers between devices: 0.11 us -> 12.9 us
    all_gather x1 -> x0, blocking collectives: 40.4 us -> none  [per_device(): lax.all_gather(v_head, 'seq', axis=0, tiled=True)]
    all_gather x1, waiting for transfers between devices: 37.2 us -> 59.9 us  [per_device(): lax.all_gather(do_head, 'seq', axis=0, tiled=True)]
    all_to_all x0 -> x1, starting transfers between devices: none -> 12.8 us  [per_device(): lax.all_to_all(jnp.stack([v_head] * lax.axis_size('seq')), 'seq', 0, 0)]
  transfers between devices with their start and end apart: 3 -> 4, of which waited for: 2 -> 2; matrix products, arithmetic and copies ran while one was open for 9% -> 10% of each run, Pallas kernels for 0% -> 0%
where the time goes in v1:
time: 992 us; the launch traced here: 988 us
  blocking collectives  564 us (57%)
  waiting for transfers between devices  147 us (15%)
  matrix products  140 us (14%)
  local copies, waits for them, and re-layouts  83.5 us (8%)
  other arithmetic  25.6 us (3%)
  between operations  14 us (1%)
  starting transfers between devices  12.9 us (1%)
    psum x1, blocking collectives, per_device(): whole_sums = lax.psum((query_part, key_part, value_part), 'seq')  140 us
    dot_general x138, matrix products, product(): jnp.einsum(pattern, former, latter, preferred_element_type=jnp.float32)  140 us
    psum x1, blocking collectives, per_device(): head_delta = lax.psum(part_delta, 'seq')  129 us
    psum x1, blocking collectives, per_device(): lax.psum(part_totals * jnp.exp(part_highest - head_highest), 'seq')  128 us
    pmax x1, blocking collectives, per_device(): lax.pmax(part_highest.astype(jnp.bfloat16), 'seq')  124 us
    psum x1, waiting for transfers between devices, per_device(): whole_sums = lax.psum((query_part, key_part, value_part), 'seq')  85.3 us
    all_gather x1, waiting for transfers between devices, per_device(): lax.all_gather(do_head, 'seq', axis=0, tiled=True)  59.9 us
    all_gather x1, blocking collectives, per_device(): lax.all_gather(k_head, 'seq', axis=0, tiled=True)  42.9 us
  transfers between devices with their start and end apart: 4, of which 2 were waited for; matrix products, arithmetic and copies ran while one was open for 10% of the time, Pallas kernels for 0%

profile of v1, /device:TPU:1, one launch (start us, length us, event | category | flops | bytes accessed | tf_op | source)
XLA Modules:
  0.0 987.9 jit_solution(4535811208277397065)
XLA Ops:
  7.9 1.4 stack.2
  9.3 12.8 %all-to-all-start = ((bf16[32,32,128]{2,1,0:T(8,128)(2,1)}), bf16[32,32,128]{2,1,0:T(8,128)(2,1)}, u32[]{:S(2)}, u32[]{:S(2)}) async-start(bf16[32,32,128]{2,1,0:T(8,128)(2,1)} %stack.2), calls=%async_computation | async-start | bytes 524288 | tf_op jit(solution)/shard_map/all_to_all | solution.py:79
  23.7 42.9 %all_gather.9 = bf16[1024,128]{1,0:T(8,128)(2,1)S(1)} all-gather(bf16[32,128]{1,0:T(8,128)(2,1)} %param.26), channel_id=1, replica_groups=mesh['seq'=32,'head'=8] {'seq'}, dimensions={0}, use_global_device_ids=true | all-gather | bytes 270336 | tf_op jit(solution)/shard_map/all_gather | solution.py:77
  68.7 9.2 while.74
  85.3 2.1 exponential_reduce_fusion.1
  87.4 3.5 fusion.95
  91.6 16.5 %while.75 = (s32[]{:T(128)}, f32[8,1,8,256]{3,2,1,0:T(8,128)}, pred[8,256]{1,0:T(8,128)(4,1)S(1)}, bf16[8,128,1,128]{3,1,2,0:T(8,128)(2,1)S(1)}, bf16[256,1,8,12...) while((s32[]{:T(128)}, f32[8,1,8,256]{3,2,1,0:T(8,128)}, ...), condition=%wide.region_11.12_spmd, body=%wide.region_9.11_spmd.sunk | while | flops 135526400 | bytes 3245173 | solution.py:133
  108.1 1.4 reduce_sum.103
  110.3 2.2 copy.93
  112.5 1.9 copy.63
  114.5 59.9 %all-gather.5.cloned.1.call-done = bf16[1024,1024]{1,0:T(8,128)(2,1)} async-done(((bf16[32,1024]{1,0:T(8,128)(2,1)}), bf16[1024,1024]{1,0:T(8,128)(2,1)}) %all-gather.5.cloned.1.call-update) | async-done | bytes 2097168 | tf_op jit(solution)/shard_map/all_gather | solution.py:84
  174.4 2.2 copy.94
  176.6 1.9 copy.64
  179.7 18.8 %while.76 = (s32[]{:T(128)}, f32[8,1,8,128]{3,2,1,0:T(8,128)}, f32[8,1,8,128]{3,2,1,0:T(8,128)}, bf16[8,128,1,8,128]{4,1,3,2,0:T(8,128)(2,1)}, bf16[256,1,128]{2,0,1:T(8,128)(2,1)S(1)}, /*index=5*/s32[]{:T(128)}) while((s32[]{:T(128)}, f32[8,1,8,128]{3,2,1,0:T(8,128)}, f32[8,1,8,128]{3,2,1,0:T(8,128)}, ...), condition=%wide.region_18.19_spmd, body=%wide.region_15.18_spmd.sunk | while | flops 68155392 | bytes 2453589 | solution.py:168
  179.7 1.3 fusion.227
  182.0 1.4 fusion.227
  184.4 1.4 fusion.227
  186.7 1.4 fusion.227
  189.1 1.4 fusion.227
  191.4 1.4 fusion.227
  193.8 1.4 fusion.227
  196.1 1.4 fusion.227
  198.5 1.4 fusion.156
  199.9 1.5 dynamic_update_slice.41
  201.3 1.5 dynamic_update_slice.40
  202.8 1.4 convert_element_type.50
  204.2 124.3 %pmax.7 = bf16[1,8,1024]{2,1,0:T(8,128)(2,1)} all-reduce(bf16[1,8,1024]{2,1,0:T(8,128)(2,1)} %convert_element_type.50), channel_id=1, replica_groups=mesh['seq'=32,'head'=8] {'seq'}, use_global_device_ids=true, to_apply=%region_20.21 | all-reduce | flops 8192 | bytes 32768 | tf_op jit(solution)/shard_map/pmax | solution.py:177
  328.5 1.4 fusion.147
  329.9 128.5 %psum.35 = f32[1,8,1024]{2,1,0:T(8,128)} all-reduce(f32[1,8,1024]{2,1,0:T(8,128)} %fusion.147), channel_id=1, replica_groups=mesh['seq'=32,'head'=8] {'seq'}, use_global_device_ids=true, to_apply=%region_22.23 | all-reduce | flops 8192 | bytes 65536 | tf_op jit(solution)/shard_map/psum | solution.py:178
  460.4 31.5 %while.77 = (s32[]{:T(128)}, f32[8,1,8,128]{3,2,1,0:T(8,128)}, bf16[8,128,1,8,128]{4,1,3,2,0:T(8,128)(2,1)}, bf16[256,1,128]{2,0,1:T(8,128)(2,1)S(1)}, f32[8,1,8...) while((s32[]{:T(128)}, f32[8,1,8,128]{3,2,1,0:T(8,128)}, ...), condition=%wide.region_25.26_spmd, body=%wide.region_23.25_spmd.sunk | while | flops 135265280 | bytes 2777197 | solution.py:183
  462.4 1.4 fusion.233
  466.3 1.4 fusion.233
  470.2 1.4 fusion.233
  474.2 1.4 fusion.233
  478.1 1.4 fusion.233
  482.0 1.4 fusion.233
  486.0 1.4 fusion.233
  489.9 1.4 fusion.233
  491.9 2.6 multiply_reduce_fusion
  494.5 1.4 bitcast_add_fusion.1
  495.8 1.5 dynamic_update_slice.42
  497.3 128.6 %psum.36 = f32[1,8,1024]{2,1,0:T(8,128)} all-reduce(f32[1,8,1024]{2,1,0:T(8,128)} %dynamic_update_slice.42), channel_id=1, replica_groups=mesh['seq'=32,'head'=8] {'seq'}, use_global_device_ids=true, to_apply=%region_27.28 | all-reduce | flops 8192 | bytes 65536 | tf_op jit(solution)/shard_map/psum | solution.py:194
  625.9 63.3 %while.79 = (s32[]{:T(128)}, f32[256,1,128]{0,2,1:T(8,128)}, f32[256,1,128]{0,2,1:T(8,128)}, f32[8,128,1,8,128]{4,3,1,0,2:T(8,128)}, bf16[8,128,1,8,128]{4,1,3,2...) while((s32[]{:T(128)}, f32[256,1,128]{0,2,1:T(8,128)}, ...), condition=%wide.region_29.30_spmd.clone, body=%wide.region_28.29_spmd.clone.sunk | while | flops 337412096 | bytes 9134296 | solution.py:205
  627.9 1.9 fusion.262
  635.8 1.9 fusion.262
  642.4 1.3 fusion.259
  643.7 1.9 fusion.262
  650.3 1.3 fusion.259
  651.6 1.9 fusion.262
  659.5 1.9 fusion.262
  667.5 1.9 fusion.262
  675.4 1.9 fusion.262
  683.3 1.9 fusion.262
  689.2 5.1 copy.140
  695.0 39.1 %while.78 = (s32[]{:T(128)}, f32[256,1,8,128]{0,3,2,1:T(8,128)}, f32[8,128,1,128]{3,1,2,0:T(8,128)}, f32[8,128,1,128]{3,1,2,0:T(8,128)}, bf16[8,128,1,128]{3,1,2...) while((s32[]{:T(128)}, f32[256,1,8,128]{0,3,2,1:T(8,128)}, ...), condition=%wide.region_14.15_spmd.clone, body=%wide.region_13.14_spmd.clone.sunk | while | flops 338182144 | bytes 17548512 | solution.py:145
  734.1 2.5 copy.79
  736.6 2.1 fusion.114
  738.7 1.4 convolution_multiply_fusion.8
  740.1 2.5 copy.56
  742.7 2.6 add_convert_fusion
  749.5 140.1 %all-reduce.5 = (bf16[1024,128]{1,0:T(8,128)(2,1)S(1)}, bf16[1024,128]{1,0:T(8,128)(2,1)}) all-reduce(f32[1024,128]{1,0:T(8,128)} %fusion.104, f32[1024,128]{1,0:T(8,128)} %fusion.105), channel_id=1, replica_groups=mesh['seq'=32,'head'=8] {'seq'}, use_global_device_ids=true, to_apply=%region_31.32 | all-reduce | flops 262144 | bytes 1572864 | tf_op jit(solution)/shard_map/psum | solution.py:218
  890.9 2.4 fusion.111
  894.5 85.3 %all-reduce.4.cloned.1.call-done = f32[1024,1024]{1,0:T(8,128)} async-done(((f32[1024,1024]{1,0:T(8,128)}), f32[1024,1024]{1,0:T(8,128)}) %all-reduce.4.cloned.1.call-update) | async-done | bytes 4194320 | tf_op jit(solution)/shard_map/psum | solution.py:218
  979.8 1.6 fusion.134
  (354 shorter events, 161.2 us)
Async XLA Ops:
  7.2 103.2 %all-gather.3.cloned.1.call-start = ((), (), s32[]{:S(2)}) async-start(), calls=%async_computation.1 | async-start | bytes 2162688 | tf_op jit(solution)/shard_map/all_gather | solution.py:83
  9.3 81.7 %all-to-all-start = ((bf16[32,32,128]{2,1,0:T(8,128)(2,1)}), bf16[32,32,128]{2,1,0:T(8,128)(2,1)}, u32[]{:S(2)}, u32[]{:S(2)}) async-start(bf16[32,32,128]{2,1,0:T(8,128)(2,1)} %stack.2), calls=%async_computation | async-start | bytes 524288 | tf_op jit(solution)/shard_map/all_to_all | solution.py:79
  22.1 152.2 %all-gather.5.cloned.1.call-start = ((), (), s32[]{:S(2)}) async-start(), calls=%async_computation.2 | async-start | bytes 2162688 | tf_op jit(solution)/shard_map/all_gather | solution.py:84
  22.9 956.9 %all-reduce.4.cloned.1.call-start = ((), (), s32[]{:S(2)}) async-start(), calls=%async_computation.3 | async-start | bytes 8388608 | tf_op jit(solution)/shard_map/psum | solution.py:218
  68.7 9.2 copy-start.2
  68.7 9.2 copy-start.13
  78.4 1.9 copy-start.21
  78.4 4.6 copy-start.8
  79.0 1.3 copy-start.22
  79.0 2.6 copy-start.15
  81.7 5.8 copy-start.4
  83.0 8.0 copy-start.23
  108.1 1.5 copy-start.18
  459.1 1.3 copy-start.17
  626.6 4.5 copy-start.5
  632.3 1.4 copy-start.6
  634.5 4.5 copy-start.5
  640.2 1.4 copy-start.6
  642.4 4.5 copy-start.5
  648.2 1.4 copy-start.6
  650.3 4.5 copy-start.5
  656.1 1.4 copy-start.6
  658.2 4.5 copy-start.5
  664.0 1.4 copy-start.6
  666.1 4.5 copy-start.5
  671.9 1.4 copy-start.6
  674.1 4.5 copy-start.5
  679.8 1.4 copy-start.6
  682.0 4.5 copy-start.5
  687.7 1.4 copy-start.6
  694.3 0.7 copy-start.19
  695.3 3.0 copy-start
  698.8 1.1 copy-start.1
  700.2 3.0 copy-start
  703.7 1.1 copy-start.1
  705.1 3.0 copy-start
  708.6 1.1 copy-start.1
  710.0 3.0 copy-start
  713.5 1.1 copy-start.1
  714.9 3.0 copy-start
  718.4 1.1 copy-start.1
  719.8 3.0 copy-start
  723.2 1.1 copy-start.1
  724.7 3.0 copy-start
  728.1 1.1 copy-start.1
  729.6 3.0 copy-start
  733.0 1.1 copy-start.1
  734.1 2.5 copy-start.20
  738.7 1.4 copy-start.11
  740.1 6.0 copy-start.24
  742.7 3.5 copy-start.3
  742.7 3.5 copy-start.12
  745.3 1.5 copy-start.16
  745.3 1.5 copy-start.26
  746.4 1.6 copy-start.14
  746.5 1.6 copy-start.25
  746.9 2.4 copy-start.7
  746.9 2.5 copy-start.10
  749.3 144.1 %copy-start.9 = (bf16[256,1024]{1,0:T(8,128)(2,1)S(1)}, bf16[256,1024]{1,0:T(8,128)(2,1)}, u32[]{:S(2)}) copy-start(bf16[256,1024]{1,0:T(8,128)(2,1)} %param.24) | copy-start | bytes 1572868
Sparse Core Ops, SparseCore 0:
  10.8 84.1 all-gather.2
  97.8 76.5 all-gather.4
  694.4 285.2 all-reduce.3
